TPU v7x, 32 devices: a whole 2x2x4 slice. The times are simulated.
32 devices in a mesh: gx: 8 (over z, x), gy: 4 (over y, core).
Axes of the slice: x: 2, y: 2, z: 4, core: 2. Of those that a mesh axis runs over, the one named last changes fastest.
Arguments:
- control: float32 [75, 128, 1024], P(None, 'gy', 'gx'), may hold values from -6 to 6
- east_coeff: float32 [75, 128, 1024], P(None, 'gy', 'gx'), may hold values from 0.12 to 0.245
- north_coeff: float32 [75, 128, 1024], P(None, 'gy', 'gx'), may hold values from 0.12 to 0.245
- ocean_mask: int32 [75, 128, 1024], P(None, 'gy', 'gx'), may hold values 0 or 1
- corner_cells: int32 [4, 131072], P(None, ('gx', 'gy')), may hold values from 0 to 4095, as said below
- corner_weights: float32 [4, 131072], P(None, ('gx', 'gy')), may hold values from 0 to 1, as said below
- obs_value: float32 [75, 131072], P(None, ('gx', 'gy')), may hold values from -6 to 6
- obs_precision: float32 [75, 131072], P(None, ('gx', 'gy')), may hold values from 0.3 to 3
- slot_counts: int32 [32, 32], P(('gx', 'gy')), may hold values from 1 to 128, as said below
Outputs:
- gradient: float32 [75, 128, 1024], P(None, 'gy', 'gx')
- departures: float32 [75, 131072], P(None, ('gx', 'gy'))
Inputs may be any that keep to these rules, and one draw needn't show every extreme that they name: For each slot, corner_cells lists the cells (r, s), (r, s + 1), (r + 1, s), (r + 1, s + 1) of one grid cell with r < 31 and s < 127, numbered r * 128 + s in the holding device's tile, in that order. `corner_weights`: the four weights of a slot are the bilinear weights (1 - a)(1 - b), a(1 - b), (1 - a)b, ab of two fractions a, b in [0, 1]; they sum to 1. slot_counts[d, p] counts the live slots that device p holds for owner d; for every owner some device sends exactly 128 live slots.
All inputs are finite; a program needn't handle non-finite values. No bound on the sum of `ocean_mask` on one device may be relied on, other than what follows from the above.
Results may differ from a plain program's by a relative error of at most 0.00002.
Values sent between devices are 32-bit elements; how exact they have to be, the bound alone decides.
No kernel may reach another device: no remote copies, remote signals or barrier semaphores. Data moves between devices by JAX's collectives and lax.ppermute only.
A program may use at most 128 MiB of HBM per device.

v0:
```python
import jax
import jax.numpy as jnp
from jax import lax
from jax.sharding import PartitionSpec as P

STEPS = 4


def with_halo(x, sides, width):
    for axis, dim in sides:
        size, length = (lax.axis_size(axis), x.shape[dim])
        up = [(i, (i + 1) % size) for i in range(size)]
        down = [(j, i) for i, j in up]
        last = lax.slice_in_dim(x, length - width, length, axis=dim)
        first = lax.slice_in_dim(x, 0, width, axis=dim)
        before = lax.ppermute(last, axis, up)
        after = lax.ppermute(first, axis, down)
        x = jnp.concatenate([before, x, after], axis=dim)
    return x


def sweep(padded, east, north):
    centre = padded[:, 1:-1, 1:-1]
    return (
        centre
        + east[:, 1:-1, 1:-1] * (padded[:, 1:-1, 2:] - centre)
        - east[:, 1:-1, :-2] * (centre - padded[:, 1:-1, :-2])
        + north[:, 1:-1, 1:-1] * (padded[:, 2:, 1:-1] - centre)
        - north[:, :-2, 1:-1] * (centre - padded[:, :-2, 1:-1])
    )


def body(
    control,
    east_coeff,
    north_coeff,
    ocean_mask,
    corner_cells,
    corner_weights,
    obs_value,
    obs_precision,
    slot_counts,
):
    levels, tile_rows, tile_cols = control.shape
    lat_index = lax.axis_index("gy")
    total_rows = tile_rows * lax.axis_size("gy")
    masked = ocean_mask.astype(jnp.float32)
    stacked = jnp.stack([masked, east_coeff, north_coeff])
    margin = STEPS
    rimmed = with_halo(stacked, (("gx", 3), ("gy", 2)), STEPS)
    mask_wide = rimmed[0]
    east = rimmed[1][:, :, :-1] * mask_wide[:, :, :-1] * mask_wide[:, :, 1:]
    east = jnp.pad(east, ((0, 0), (0, 0), (0, 1)))
    north = rimmed[2][:, :-1, :] * mask_wide[:, :-1, :] * mask_wide[:, 1:, :]
    global_rows = lat_index * tile_rows - margin + jnp.arange(tile_rows + 2 * margin - 1)
    row_keep = ((global_rows >= 0) & (global_rows < total_rows - 1)).astype(jnp.float32)
    north = jnp.pad(north * row_keep[None, :, None], ((0, 0), (0, 1), (0, 0)))

    def diffuse(current):
        padded = with_halo(current, (("gx", 2), ("gy", 1)), STEPS)
        for sweep_count in range(STEPS):
            remain = STEPS - sweep_count
            height = tile_rows + 2 * remain
            width_now = tile_cols + 2 * remain
            padded = sweep(
                padded,
                east[:, sweep_count : sweep_count + height, sweep_count : sweep_count + width_now],
                north[:, sweep_count : sweep_count + height, sweep_count : sweep_count + width_now],
            )
        return padded

    background = diffuse(masked * control)
    flat = background.reshape(levels, -1)
    corners = corner_cells.shape[0]
    cell_list = corner_cells.reshape(-1)
    picked = jnp.take(flat, cell_list, axis=1).reshape(levels, corners, -1)
    equivalent = jnp.sum(picked * corner_weights[None, :, :], axis=1)
    slots = equivalent.shape[1]
    peers = lax.axis_size(("gx", "gy"))
    capacity = slots // peers
    received = lax.all_to_all(equivalent, ("gx", "gy"), split_axis=1, concat_axis=1, tiled=True)
    live = (slot_counts[0][:, None] > jnp.arange(capacity)[None, :]).reshape(slots)
    departures = jnp.where(live[None, :], obs_precision * (received - obs_value), jnp.float32(0.0))
    returned = lax.all_to_all(departures, ("gx", "gy"), split_axis=1, concat_axis=1, tiled=True)
    spread = (corner_weights[None, :, :] * returned[:, None, :]).reshape(levels, -1)
    adjoint = jnp.zeros((levels, tile_rows * tile_cols), jnp.float32).at[:, cell_list].add(spread)
    gradient = masked * (control + diffuse(adjoint.reshape(levels, tile_rows, tile_cols)))
    return (gradient, departures)


def solution(mesh):
    return jax.shard_map(
        body,
        mesh=mesh,
        in_specs=(
            P(None, "gy", "gx"),
            P(None, "gy", "gx"),
            P(None, "gy", "gx"),
            P(None, "gy", "gx"),
            P(None, ("gx", "gy")),
            P(None, ("gx", "gy")),
            P(None, ("gx", "gy")),
            P(None, ("gx", "gy")),
            P(("gx", "gy"), None),
        ),
        out_specs=(P(None, "gy", "gx"), P(None, ("gx", "gy"))),
        check_vma=False,
    )
```

profile of v0, /device:TPU:1, one launch (start us, length us, event | category | flops | bytes accessed | tf_op | source)
XLA Modules:
  0.0 347.6 jit_solution(17975862376519627742)
XLA Ops:
  0.6 2.4 copy.75
  7.4 3.1 copy.82
  14.4 3.0 collective-permute-start.5
  19.6 2.2 convert_multiply_fusion
  21.9 4.1 %collective-permute-start.1 = (f32[75,32,4]{0,1,2:T(8,128)S(1)}, f32[75,32,4]{0,1,2:T(8,128)S(1)}, u32[]{:S(2)}, u32[]{:S(2)}) collective-permute-start(f32[75,32,4]{0,1,2:T(8,128)S(1)} %get-tuple-element.24), channel_id=1, source_target_pairs={{4,0},{8,4},{12,8},{16,12},{20,16},{24,20},{28,24},{0,28},{5,1},{9... | collective-permute-start | bytes 115208 | tf_op jit(solution)/shard_map/ppermute | solution.py:17
  27.9 3.5 collective-permute-start.2
  37.8 3.0 collective-permute-done.3
  41.9 2.3 pad_maximum_fusion.1
  44.2 10.0 %collective-permute-done.6 = f32[3,75,4,136]{1,3,2,0:T(8,128)} collective-permute-done((f32[3,75,4,136]{1,3,2,0:T(8,128)S(1)}, f32[3,75,4,136]{1,3,2,0:T(8,128)}, u32[]{:S(2)}, u32[]{:S(2)}) %collective-permute-start.6) | collective-permute-done | bytes 489632 | tf_op jit(solution)/shard_map/ppermute | solution.py:16
  57.7 4.9 %pad_maximum_fusion = f32[3,75,40,136]{1,2,3,0:T(8,128)S(1)} fusion(f32[3,75,4,136]{1,2,3,0:T(4,128)S(1)} %copy.86, f32[3,75,32,4]{1,2,3,0:T(8,128)} %collective-permute-done.5, f32[1,75,32,128]{1,2,3,0:T(8,128)S(1)} %bitcast.45, f32[1,75,32,128]{1,2,3,0:T(8,128)S(1)} %bitcast.42, f32[1,75,32,128]{1,2,3,0:T(8,128)S(1)} %copy-done.6, ...), kind=kLoop, calls=%fused_computation.6 | loop fusion | flops 7344000 | bytes 9792000 | tf_op jit(solution)/shard_map/concatenate | solution.py:18
  64.0 3.1 fusion.12
  67.2 3.1 fusion.28
  70.3 3.1 fusion.44
  76.9 54.8 %gather_fusion = f32[16384,75]{1,0:T(8,128)} fusion(f32[75,4096]{0,1:T(8,128)S(1)} %bitcast.39, s32[16384]{0:T(1024)S(1)} %copy-done.19), kind=kCustom, calls=%fused_computation | custom fusion | bytes 9895936 | tf_op jit(solution)/shard_map/jit(_take)/gather | solution.py:76
  131.6 6.9 %multiply_reduce_fusion = f32[75,4096]{0,1:T(8,128)S(1)} fusion(f32[75,4,4096]{0,2,1:T(8,128)} %bitcast.46, f32[4,4096]{1,0:T(4,128)S(1)} %copy-done.18, pred[4,4096]{1,0:T(4,128)(4,1)S(1)} %compare_and_fusion), kind=kLoop, calls=%fused_computation.5 | loop fusion | flops 3379200 | bytes 6225920 | tf_op jit(solution)/shard_map/reduce_sum | solution.py:77
  140.3 6.5 %all-to-all-start = ((f32[75,32,128]{2,0,1:T(8,128)}), f32[75,32,128]{2,0,1:T(8,128)S(1)}, u32[]{:S(2)}, u32[]{:S(2)}) async-start(f32[75,32,128]{2,0,1:T(8,128)} %copy.89), calls=%async_computation | async-start | bytes 2621440 | tf_op jit(solution)/shard_map/all_to_all | solution.py:81
  148.7 2.8 copy.92
  151.6 26.1 %all-to-all-done = f32[75,32,128]{2,0,1:T(8,128)S(1)} async-done(((f32[75,32,128]{2,0,1:T(8,128)}), f32[75,32,128]{2,0,1:T(8,128)S(1)}, u32[]{:S(2)}, u32[]{:S(2)}) %all-to-all-start) | async-done | bytes 1228832 | tf_op jit(solution)/shard_map/all_to_all | solution.py:81
  179.5 3.2 fusion.70
  184.4 4.6 %all-to-all-start.1 = ((f32[75,32,128]{2,0,1:T(8,128)}), f32[75,32,128]{2,0,1:T(8,128)S(1)}, u32[]{:S(2)}, u32[]{:S(2)}) async-start(f32[75,32,128]{2,0,1:T(8,128)} %copy.93), calls=%async_computation.1 | async-start | bytes 2621440 | tf_op jit(solution)/shard_map/all_to_all | solution.py:84
  189.0 30.8 %all-to-all-done.1 = f32[75,32,128]{2,0,1:T(8,128)S(1)} async-done(((f32[75,32,128]{2,0,1:T(8,128)}), f32[75,32,128]{2,0,1:T(8,128)S(1)}, u32[]{:S(2)}, u32[]{:S(2)}) %all-to-all-start.1) | async-done | bytes 1228832 | tf_op jit(solution)/shard_map/all_to_all | solution.py:84
  221.6 6.0 %bitcast_multiply_fusion = f32[75,16384]{0,1:T(8,128)} fusion(f32[75,4096]{0,1:T(8,128)} %bitcast.51, f32[16384]{0:T(1024)S(1)} %bitcast.53), kind=kLoop, calls=%fused_computation.4 | loop fusion | flops 1228800 | bytes 6209536 | tf_op jit(solution)/shard_map/mul | solution.py:85
  227.6 81.0 %scatter_custom_fusion = f32[75,4096]{0,1:T(8,128)} fusion(s32[16384]{0:T(1024)} %bitcast.56, f32[75,16384]{0,1:T(8,128)} %bitcast_multiply_fusion, f32[]{:T(128)} %constant.9.clone.1), kind=kCustom, calls=%fused_computation.2 | custom fusion | flops 1228800 | bytes 9617920 | tf_op jit(solution)/shard_map/scatter-add | solution.py:86
  311.1 2.8 collective-permute-start.9
  315.6 2.8 constant_dynamic-update-slice_fusion.1
  319.9 3.5 %collective-permute-start.10 = (f32[75,4,136]{0,2,1:T(8,128)S(1)}, f32[75,4,136]{0,2,1:T(8,128)S(1)}, u32[]{:S(2)}, u32[]{:S(2)}) collective-permute-start(f32[75,4,136]{0,2,1:T(8,128)S(1)} %copy.99), channel_id=1, source_target_pairs={{0,1},{1,2},{2,3},{3,0},{4,5},{5,6},{6,7},{7,4},{8,9},{9,10},{10,1... | collective-permute-start | bytes 489608 | tf_op jit(solution)/shard_map/ppermute | solution.py:16
  325.5 3.2 collective-permute-done.10
  330.7 2.3 pad_maximum_fusion.2
  334.0 2.9 fusion.4
  336.9 3.0 fusion.20
  340.0 3.0 fusion.36
  343.0 2.6 fusion.54
  (106 shorter events, 49.6 us)
Async XLA Ops:
  3.0 16.6 %copy-start.4 = (s32[75,32,128]{0,1,2:T(8,128)}, s32[75,32,128]{0,1,2:T(8,128)S(1)}, u32[]{:S(2)}) copy-start(s32[75,32,128]{0,1,2:T(8,128)S(1)} %copy.75) | copy-start | bytes 3686404
  10.5 7.0 %copy-start.16 = (f32[75,32,128]{2,1,0:T(8,128)S(1)}, f32[75,32,128]{2,1,0:T(8,128)}, u32[]{:S(2)}) copy-start(f32[75,32,128]{2,1,0:T(8,128)} %param.9) | copy-start | bytes 3686404
  12.4 19.7 %collective-permute-start.4 = (f32[3,75,32,4]{1,2,3,0:T(8,128)}, f32[3,75,32,4]{1,2,3,0:T(8,128)S(1)}, u32[]{:S(2)}, u32[]{:S(2)}) collective-permute-start(f32[3,75,32,4]{1,2,3,0:T(8,128)} %get-tuple-element.15), channel_id=1, source_target_pairs={{0,4},{4,8},{8,12},{12,16},{16,20},{20,24},{24,28},{28,0},{1,5},{5... | collective-permute-start | bytes 345608 | tf_op jit(solution)/shard_map/ppermute | solution.py:16
  14.4 17.7 %collective-permute-start.5 = (f32[3,75,32,4]{1,2,3,0:T(8,128)}, f32[3,75,32,4]{1,2,3,0:T(8,128)}, u32[]{:S(2)}, u32[]{:S(2)}) collective-permute-start(f32[3,75,32,4]{1,2,3,0:T(8,128)} %get-tuple-element.16), channel_id=1, source_target_pairs={{4,0},{8,4},{12,8},{16,12},{20,16},{24,20},{28,24},{0,28},{5,1},{9... | collective-permute-start | bytes 345608 | tf_op jit(solution)/shard_map/ppermute | solution.py:17
  19.6 6.5 %copy-start.20 = (s32[4,4096]{1,0:T(4,128)S(1)}, s32[4,4096]{1,0:T(4,128)}, u32[]{:S(2)}) copy-start(s32[4,4096]{1,0:T(4,128)} %param.13) | copy-start | bytes 196612
  19.6 12.5 %copy-start.9 = (f32[75,32,128]{0,1,2:T(8,128)S(1)}, f32[75,32,128]{0,1,2:T(8,128)}, u32[]{:S(2)}) copy-start(f32[75,32,128]{0,1,2:T(8,128)} %copy.82) | copy-start | bytes 3686404
  21.8 5.9 %copy-start.11 = (f32[75,32,128]{0,1,2:T(8,128)}, f32[75,32,128]{0,1,2:T(8,128)S(1)}, u32[]{:S(2)}) copy-start(f32[75,32,128]{0,1,2:T(8,128)S(1)} %convert_multiply_fusion) | copy-start | bytes 3686404
  21.8 10.3 %copy-start.6 = (f32[1,75,32,128]{1,2,3,0:T(8,128)S(1)}, f32[1,75,32,128]{1,2,3,0:T(8,128)}, u32[]{:S(2)}) copy-start(f32[1,75,32,128]{1,2,3,0:T(8,128)} %convert_bitcast_fusion) | copy-start | bytes 3686404
  21.8 10.3 %copy-start.7 = (f32[75,32,128]{0,1,2:T(8,128)S(1)}, f32[75,32,128]{0,1,2:T(8,128)}, u32[]{:S(2)}) copy-start(f32[75,32,128]{0,1,2:T(8,128)} %copy.81) | copy-start | bytes 3686404
  21.9 5.9 %collective-permute-start = (f32[75,32,4]{0,1,2:T(8,128)S(1)}, f32[75,32,4]{0,1,2:T(8,128)S(1)}, u32[]{:S(2)}, u32[]{:S(2)}) collective-permute-start(f32[75,32,4]{0,1,2:T(8,128)S(1)} %get-tuple-element.23), channel_id=1, source_target_pairs={{0,4},{4,8},{8,12},{12,16},{16,20},{20,24},{24,28},{28,0},{1,5},{5... | collective-permute-start | bytes 115208 | tf_op jit(solution)/shard_map/ppermute | solution.py:16
  21.9 5.8 %collective-permute-start.1 = (f32[75,32,4]{0,1,2:T(8,128)S(1)}, f32[75,32,4]{0,1,2:T(8,128)S(1)}, u32[]{:S(2)}, u32[]{:S(2)}) collective-permute-start(f32[75,32,4]{0,1,2:T(8,128)S(1)} %get-tuple-element.24), channel_id=1, source_target_pairs={{4,0},{8,4},{12,8},{16,12},{20,16},{24,20},{28,24},{0,28},{5,1},{9... | collective-permute-start | bytes 115208 | tf_op jit(solution)/shard_map/ppermute | solution.py:17
  26.2 9.9 %copy-start.21 = (s32[16384,1]{0,1:T(1,128)}, s32[16384,1]{0,1:T(1,128)S(1)}, u32[]{:S(2)}) copy-start(s32[16384,1]{0,1:T(1,128)S(1)} %compare_select_fusion) | copy-start | bytes 196612
  27.7 5.6 %copy-start.17 = (f32[75,32,4]{0,1,2:T(8,128)}, f32[75,32,4]{0,1,2:T(8,128)S(1)}, u32[]{:S(2)}) copy-start(f32[75,32,4]{0,1,2:T(8,128)S(1)} %collective-permute-done.1) | copy-start | bytes 115204
  27.9 8.9 %collective-permute-start.2 = (f32[75,4,136]{0,2,1:T(8,128)S(1)}, f32[75,4,136]{0,2,1:T(8,128)}, u32[]{:S(2)}, u32[]{:S(2)}) collective-permute-start(f32[75,4,136]{0,2,1:T(8,128)S(1)} %copy.77), channel_id=1, source_target_pairs={{0,1},{1,2},{2,3},{3,0},{4,5},{5,6},{6,7},{7,4},{8,9},{9,10},{10,1... | collective-permute-start | bytes 489608 | tf_op jit(solution)/shard_map/ppermute | solution.py:16
  32.1 8.8 %collective-permute-start.3 = (f32[75,4,136]{0,2,1:T(8,128)}, f32[75,4,136]{0,2,1:T(8,128)}, u32[]{:S(2)}, u32[]{:S(2)}) collective-permute-start(f32[75,4,136]{0,2,1:T(8,128)} %copy.78), channel_id=1, source_target_pairs={{1,0},{2,1},{3,2},{0,3},{5,4},{6,5},{7,6},{4,7},{9,8},{10,9},{11,1... | collective-permute-start | bytes 489608 | tf_op jit(solution)/shard_map/ppermute | solution.py:17
  33.4 20.8 %collective-permute-start.6 = (f32[3,75,4,136]{1,3,2,0:T(8,128)S(1)}, f32[3,75,4,136]{1,3,2,0:T(8,128)}, u32[]{:S(2)}, u32[]{:S(2)}) collective-permute-start(f32[3,75,4,136]{1,3,2,0:T(8,128)S(1)} %copy.83), channel_id=1, source_target_pairs={{0,1},{1,2},{2,3},{3,0},{4,5},{5,6},{6,7},{7,4},{8,9},{9,10},{10,1... | collective-permute-start | bytes 1468808 | tf_op jit(solution)/shard_map/ppermute | solution.py:16
  36.2 20.2 %collective-permute-start.7 = (f32[3,75,4,136]{1,3,2,0:T(8,128)}, f32[3,75,4,136]{1,3,2,0:T(8,128)}, u32[]{:S(2)}, u32[]{:S(2)}) collective-permute-start(f32[3,75,4,136]{1,3,2,0:T(8,128)} %copy.84), channel_id=1, source_target_pairs={{1,0},{2,1},{3,2},{0,3},{5,4},{6,5},{7,6},{4,7},{9,8},{10,9},{11,1... | collective-permute-start | bytes 1468808 | tf_op jit(solution)/shard_map/ppermute | solution.py:17
  41.9 15.8 %copy-start.10 = (f32[75,32,128]{0,1,2:T(8,128)S(1)}, f32[75,32,128]{0,1,2:T(8,128)}, u32[]{:S(2)}) copy-start(f32[75,32,128]{0,1,2:T(8,128)} %copy.82) | copy-start | bytes 3686404
  44.2 13.5 %copy-start.8 = (f32[75,32,128]{0,1,2:T(8,128)S(1)}, f32[75,32,128]{0,1,2:T(8,128)}, u32[]{:S(2)}) copy-start(f32[75,32,128]{0,1,2:T(8,128)} %copy.81) | copy-start | bytes 3686404
  63.5 9.9 %copy-start = (f32[75,40,135]{0,1,2:T(8,128)}, f32[75,40,135]{0,1,2:T(8,128)S(1)}, u32[]{:S(2)}) copy-start(f32[75,40,135]{0,1,2:T(8,128)S(1)} %slice_multiply_fusion.2) | copy-start | bytes 4860004
  64.0 9.3 %copy-start.2 = (f32[75,39,136]{0,1,2:T(8,128)}, f32[75,39,136]{0,1,2:T(8,128)S(1)}, u32[]{:S(2)}) copy-start(f32[75,39,136]{0,1,2:T(8,128)S(1)} %fusion.2) | copy-start | bytes 4773604
  76.9 54.8 %copy-start.18 = (f32[4,4096]{1,0:T(4,128)S(1)}, f32[4,4096]{1,0:T(4,128)}, u32[]{:S(2)}) copy-start(f32[4,4096]{1,0:T(4,128)} %param.14) | copy-start | bytes 196612
  138.6 8.2 %copy-start.14 = (f32[75,4096]{1,0:T(8,128)S(1)}, f32[75,4096]{1,0:T(8,128)}, u32[]{:S(2)}) copy-start(f32[75,4096]{1,0:T(8,128)} %param.15) | copy-start | bytes 3686404
  140.3 37.3 %all-to-all-start = ((f32[75,32,128]{2,0,1:T(8,128)}), f32[75,32,128]{2,0,1:T(8,128)S(1)}, u32[]{:S(2)}, u32[]{:S(2)}) async-start(f32[75,32,128]{2,0,1:T(8,128)} %copy.89), calls=%async_computation | async-start | bytes 2621440 | tf_op jit(solution)/shard_map/all_to_all | solution.py:81
  146.8 4.7 %copy-start.22 = (s32[1,32]{1,0:T(1,128)S(1)}, s32[1,32]{1,0:T(1,128)}, u32[]{:S(2)}) copy-start(s32[1,32]{1,0:T(1,128)} %param.17) | copy-start | bytes 388
  184.4 35.4 %all-to-all-start.1 = ((f32[75,32,128]{2,0,1:T(8,128)}), f32[75,32,128]{2,0,1:T(8,128)S(1)}, u32[]{:S(2)}, u32[]{:S(2)}) async-start(f32[75,32,128]{2,0,1:T(8,128)} %copy.93), calls=%async_computation.1 | async-start | bytes 2621440 | tf_op jit(solution)/shard_map/all_to_all | solution.py:84
  309.7 5.9 %collective-permute-start.8 = (f32[75,32,4]{0,1,2:T(8,128)S(1)}, f32[75,32,4]{0,1,2:T(8,128)S(1)}, u32[]{:S(2)}, u32[]{:S(2)}) collective-permute-start(f32[75,32,4]{0,1,2:T(8,128)S(1)} %copy.113), channel_id=1, source_target_pairs={{0,4},{4,8},{8,12},{12,16},{16,20},{20,24},{24,28},{28,0},{1,5},{5... | collective-permute-start | bytes 115208 | tf_op jit(solution)/shard_map/ppermute | solution.py:16
  311.1 7.3 %collective-permute-start.9 = (f32[75,32,4]{0,1,2:T(8,128)S(1)}, f32[75,32,4]{0,1,2:T(8,128)S(1)}, u32[]{:S(2)}, u32[]{:S(2)}) collective-permute-start(f32[75,32,4]{0,1,2:T(8,128)S(1)} %copy.114), channel_id=1, source_target_pairs={{4,0},{8,4},{12,8},{16,12},{20,16},{24,20},{28,24},{0,28},{5,1},{9... | collective-permute-start | bytes 115208 | tf_op jit(solution)/shard_map/ppermute | solution.py:17
  319.9 8.8 %collective-permute-start.10 = (f32[75,4,136]{0,2,1:T(8,128)S(1)}, f32[75,4,136]{0,2,1:T(8,128)S(1)}, u32[]{:S(2)}, u32[]{:S(2)}) collective-permute-start(f32[75,4,136]{0,2,1:T(8,128)S(1)} %copy.99), channel_id=1, source_target_pairs={{0,1},{1,2},{2,3},{3,0},{4,5},{5,6},{6,7},{7,4},{8,9},{9,10},{10,1... | collective-permute-start | bytes 489608 | tf_op jit(solution)/shard_map/ppermute | solution.py:16
  323.5 7.2 %collective-permute-start.11 = (f32[75,4,136]{0,2,1:T(8,128)S(1)}, f32[75,4,136]{0,2,1:T(8,128)S(1)}, u32[]{:S(2)}, u32[]{:S(2)}) collective-permute-start(f32[75,4,136]{0,2,1:T(8,128)S(1)} %copy.100), channel_id=1, source_target_pairs={{1,0},{2,1},{3,2},{0,3},{5,4},{6,5},{7,6},{4,7},{9,8},{10,9},{11,1... | collective-permute-start | bytes 489608 | tf_op jit(solution)/shard_map/ppermute | solution.py:17
  330.7 3.3 copy-start.3
  340.0 3.0 copy-start.5
  (5 other events, 10.3 us)
where the time goes:
time: 348 us
  other arithmetic  138 us (40%)
  local copies, waits for them, and re-layouts  95.6 us (27%)
  waiting for transfers between devices  78.9 us (23%)
  starting transfers between devices  33.7 us (10%)
    scatter-add x1, other arithmetic, body(): jnp.zeros((levels, tile_rows * tile_cols), jnp.float32).at[:, cell_list]  81 us
    gather x1, local copies, waits for them, and re-layouts, body(): picked = jnp.take(flat, cell_list, axis=1).reshape(levels, corners, -1)  54.8 us
    all_to_all x1, waiting for transfers between devices, body(): lax.all_to_all(departures, ('gx', 'gy'), split_axis=1, concat_axis=1, til...  30.8 us
    all_to_all x1, waiting for transfers between devices, body(): lax.all_to_all(equivalent, ('gx', 'gy'), split_axis=1, concat_axis=1, til...  26.1 us
    unnamed x60, local copies, waits for them, and re-layouts  24.1 us
    sub x7, other arithmetic, sweep(): centre + east[:, 1:-1, 1:-1] * (padded[:, 1:-1, 2:] - centre)  20.4 us
    ppermute x6, waiting for transfers between devices, with_halo(): before = lax.ppermute(last, axis, up)  16.4 us
    ppermute x6, starting transfers between devices, with_halo(): before = lax.ppermute(last, axis, up)  12.2 us
  transfers between devices with their start and end apart: 14, of which 9 were waited for; matrix products, arithmetic and copies ran while one was open for 7% of the time, Pallas kernels for 0%

commit v1 on v0

--- a/solution.py
+++ b/solution.py
@@ -81,7 +81,9 @@
     received = lax.all_to_all(equivalent, ("gx", "gy"), split_axis=1, concat_axis=1, tiled=True)
     live = (slot_counts[0][:, None] > jnp.arange(capacity)[None, :]).reshape(slots)
     departures = jnp.where(live[None, :], obs_precision * (received - obs_value), jnp.float32(0.0))
-    returned = lax.all_to_all(departures, ("gx", "gy"), split_axis=1, concat_axis=1, tiled=True)
+    pieces = jnp.split(departures, lax.axis_size(("gx", "gy")), axis=1)
+    incoming = lax.all_to_all(jnp.stack(pieces), ("gx", "gy"), 0, 0)
+    returned = jnp.concatenate(incoming, axis=1)
     spread = (corner_weights[None, :, :] * returned[:, None, :]).reshape(levels, -1)
     adjoint = jnp.zeros((levels, tile_rows * tile_cols), jnp.float32).at[:, cell_list].add(spread)
     gradient = masked * (control + diffuse(adjoint.reshape(levels, tile_rows, tile_cols)))

time: 348 us -> 370 us (1.063)
  local copies, waits for them, and re-layouts: 95.6 us -> 117 us
    unnamed x60 -> x91, local copies, waits for them, and re-layouts: 24.1 us -> 43.6 us
  transfers between devices with their start and end apart: 14 -> 14, of which waited for: 9 -> 9; matrix products, arithmetic and copies ran while one was open for 7% -> 6% of each run, Pallas kernels for 0% -> 0%
where the time goes in v1:
time: 370 us; the launch traced here: 369 us
  other arithmetic  138 us (37%)
  local copies, waits for them, and re-layouts  117 us (32%)
  waiting for transfers between devices  78.9 us (21%)
  starting transfers between devices  33.7 us (9%)
    scatter-add x1, other arithmetic, body(): jnp.zeros((levels, tile_rows * tile_cols), jnp.float32).at[:, cell_list]  81 us
    gather x1, local copies, waits for them, and re-layouts, body(): picked = jnp.take(flat, cell_list, axis=1).reshape(levels, corners, -1)  54.8 us
    unnamed x91, local copies, waits for them, and re-layouts  43.6 us
    all_to_all x1, waiting for transfers between devices, body(): incoming = lax.all_to_all(jnp.stack(pieces), ('gx', 'gy'), 0, 0)  30.8 us
    all_to_all x1, waiting for transfers between devices, body(): lax.all_to_all(equivalent, ('gx', 'gy'), split_axis=1, concat_axis=1, til...  26.1 us
    sub x7, other arithmetic, sweep(): centre + east[:, 1:-1, 1:-1] * (padded[:, 1:-1, 2:] - centre)  20.4 us
    ppermute x6, waiting for transfers between devices, with_halo(): before = lax.ppermute(last, axis, up)  16.4 us
    ppermute x6, starting transfers between devices, with_halo(): before = lax.ppermute(last, axis, up)  12.2 us
  transfers between devices with their start and end apart: 14, of which 9 were waited for; matrix products, arithmetic and copies ran while one was open for 6% of the time, Pallas kernels for 0%

profile of v1, /device:TPU:1, one launch (start us, length us, event | category | flops | bytes accessed | tf_op | source)
XLA Modules:
  0.0 368.9 jit_solution(10406987945311123805)
XLA Ops:
  0.6 2.4 copy.75
  7.4 3.1 copy.82
  14.4 3.0 collective-permute-start.5
  21.9 4.1 %collective-permute-start.1 = (f32[75,32,4]{0,1,2:T(8,128)S(1)}, f32[75,32,4]{0,1,2:T(8,128)S(1)}, u32[]{:S(2)}, u32[]{:S(2)}) collective-permute-start(f32[75,32,4]{0,1,2:T(8,128)S(1)} %get-tuple-element.24), channel_id=1, source_target_pairs={{4,0},{8,4},{12,8},{16,12},{20,16},{24,20},{28,24},{0,28},{5,1},{9... | collective-permute-start | bytes 115208 | tf_op jit(solution)/shard_map/ppermute | solution.py:17
  27.9 3.5 collective-permute-start.2
  37.8 3.0 collective-permute-done.3
  41.9 2.3 pad_maximum_fusion.1
  44.2 10.0 %collective-permute-done.6 = f32[3,75,4,136]{1,3,2,0:T(8,128)} collective-permute-done((f32[3,75,4,136]{1,3,2,0:T(8,128)S(1)}, f32[3,75,4,136]{1,3,2,0:T(8,128)}, u32[]{:S(2)}, u32[]{:S(2)}) %collective-permute-start.6) | collective-permute-done | bytes 489632 | tf_op jit(solution)/shard_map/ppermute | solution.py:16
  57.7 4.9 %pad_maximum_fusion = f32[3,75,40,136]{1,2,3,0:T(8,128)S(1)} fusion(f32[3,75,4,136]{1,2,3,0:T(4,128)S(1)} %copy.86, f32[3,75,32,4]{1,2,3,0:T(8,128)} %collective-permute-done.5, f32[1,75,32,128]{1,2,3,0:T(8,128)S(1)} %bitcast.173, f32[1,75,32,128]{1,2,3,0:T(8,128)S(1)} %bitcast.170, f32[1,75,32,128]{1,2,3,0:T(8,128)S(1)} %copy-done.6, ...), kind=kLoop, calls=%fused_computation.6 | loop fusion | flops 7344000 | bytes 9792000 | tf_op jit(solution)/shard_map/concatenate | solution.py:18
  64.0 3.1 fusion.12
  67.2 3.1 fusion.28
  70.3 3.1 fusion.44
  76.9 54.8 %gather_fusion = f32[16384,75]{1,0:T(8,128)} fusion(f32[75,4096]{0,1:T(8,128)S(1)} %bitcast.167, s32[16384]{0:T(1024)S(1)} %copy-done.19), kind=kCustom, calls=%fused_computation | custom fusion | bytes 9895936 | tf_op jit(solution)/shard_map/jit(_take)/gather | solution.py:76
  131.6 6.9 %multiply_reduce_fusion = f32[75,4096]{0,1:T(8,128)S(1)} fusion(f32[75,4,4096]{0,2,1:T(8,128)} %bitcast.174, f32[4,4096]{1,0:T(4,128)S(1)} %copy-done.18, pred[4,4096]{1,0:T(4,128)(4,1)S(1)} %compare_and_fusion), kind=kLoop, calls=%fused_computation.5 | loop fusion | flops 3379200 | bytes 6225920 | tf_op jit(solution)/shard_map/reduce_sum | solution.py:77
  140.3 6.5 %all-to-all-start = ((f32[75,32,128]{2,0,1:T(8,128)}), f32[75,32,128]{2,0,1:T(8,128)S(1)}, u32[]{:S(2)}, u32[]{:S(2)}) async-start(f32[75,32,128]{2,0,1:T(8,128)} %copy.89), calls=%async_computation | async-start | bytes 2621440 | tf_op jit(solution)/shard_map/all_to_all | solution.py:81
  148.7 2.8 copy.92
  151.6 26.1 %all-to-all-done = f32[75,32,128]{2,0,1:T(8,128)S(1)} async-done(((f32[75,32,128]{2,0,1:T(8,128)}), f32[75,32,128]{2,0,1:T(8,128)S(1)}, u32[]{:S(2)}, u32[]{:S(2)}) %all-to-all-start) | async-done | bytes 1228832 | tf_op jit(solution)/shard_map/all_to_all | solution.py:81
  179.5 3.2 fusion.70
  202.8 2.8 copy.93
  205.6 4.6 %all-to-all-start.1 = ((f32[32,75,128]{2,1,0:T(8,128)}), f32[32,75,128]{2,1,0:T(8,128)S(1)}, u32[]{:S(2)}, u32[]{:S(2)}) async-start(f32[32,75,128]{2,1,0:T(8,128)} %copy.93), calls=%async_computation.1 | async-start | bytes 2621440 | tf_op jit(solution)/shard_map/all_to_all | solution.py:85
  210.2 30.8 %all-to-all-done.1 = f32[32,75,128]{2,1,0:T(8,128)S(1)} async-done(((f32[32,75,128]{2,1,0:T(8,128)}), f32[32,75,128]{2,1,0:T(8,128)S(1)}, u32[]{:S(2)}, u32[]{:S(2)}) %all-to-all-start.1) | async-done | bytes 1228832 | tf_op jit(solution)/shard_map/all_to_all | solution.py:85
  242.8 6.0 %bitcast_multiply_fusion = f32[75,16384]{0,1:T(8,128)} fusion(f32[75,4096]{0,1:T(8,128)} %bitcast.178, f32[16384]{0:T(1024)S(1)} %bitcast.181), kind=kLoop, calls=%fused_computation.4 | loop fusion | flops 1228800 | bytes 6209536 | tf_op jit(solution)/shard_map/mul | solution.py:87
  248.9 81.0 %scatter_custom_fusion = f32[75,4096]{0,1:T(8,128)} fusion(s32[16384]{0:T(1024)} %bitcast.184, f32[75,16384]{0,1:T(8,128)} %bitcast_multiply_fusion, f32[]{:T(128)} %constant.9.clone.1), kind=kCustom, calls=%fused_computation.2 | custom fusion | flops 1228800 | bytes 9617920 | tf_op jit(solution)/shard_map/scatter-add | solution.py:88
  332.3 2.8 collective-permute-start.9
  336.8 2.8 constant_dynamic-update-slice_fusion.33
  341.1 3.5 collective-permute-start.10
  346.7 3.2 collective-permute-done.10
  351.9 2.3 pad_maximum_fusion.2
  355.2 2.9 fusion.4
  358.1 3.0 fusion.20
  361.2 3.0 fusion.36
  364.2 2.6 fusion.54
  (138 shorter events, 70.3 us)
Async XLA Ops:
  3.0 16.6 %copy-start.4 = (s32[75,32,128]{0,1,2:T(8,128)}, s32[75,32,128]{0,1,2:T(8,128)S(1)}, u32[]{:S(2)}) copy-start(s32[75,32,128]{0,1,2:T(8,128)S(1)} %copy.75) | copy-start | bytes 3686404
  10.5 7.0 %copy-start.16 = (f32[75,32,128]{2,1,0:T(8,128)S(1)}, f32[75,32,128]{2,1,0:T(8,128)}, u32[]{:S(2)}) copy-start(f32[75,32,128]{2,1,0:T(8,128)} %param.9) | copy-start | bytes 3686404
  12.4 19.7 %collective-permute-start.4 = (f32[3,75,32,4]{1,2,3,0:T(8,128)}, f32[3,75,32,4]{1,2,3,0:T(8,128)S(1)}, u32[]{:S(2)}, u32[]{:S(2)}) collective-permute-start(f32[3,75,32,4]{1,2,3,0:T(8,128)} %get-tuple-element.15), channel_id=1, source_target_pairs={{0,4},{4,8},{8,12},{12,16},{16,20},{20,24},{24,28},{28,0},{1,5},{5... | collective-permute-start | bytes 345608 | tf_op jit(solution)/shard_map/ppermute | solution.py:16
  14.4 17.7 %collective-permute-start.5 = (f32[3,75,32,4]{1,2,3,0:T(8,128)}, f32[3,75,32,4]{1,2,3,0:T(8,128)}, u32[]{:S(2)}, u32[]{:S(2)}) collective-permute-start(f32[3,75,32,4]{1,2,3,0:T(8,128)} %get-tuple-element.16), channel_id=1, source_target_pairs={{4,0},{8,4},{12,8},{16,12},{20,16},{24,20},{28,24},{0,28},{5,1},{9... | collective-permute-start | bytes 345608 | tf_op jit(solution)/shard_map/ppermute | solution.py:17
  19.6 6.5 %copy-start.20 = (s32[4,4096]{1,0:T(4,128)S(1)}, s32[4,4096]{1,0:T(4,128)}, u32[]{:S(2)}) copy-start(s32[4,4096]{1,0:T(4,128)} %param.13) | copy-start | bytes 196612
  19.6 12.5 %copy-start.9 = (f32[75,32,128]{0,1,2:T(8,128)S(1)}, f32[75,32,128]{0,1,2:T(8,128)}, u32[]{:S(2)}) copy-start(f32[75,32,128]{0,1,2:T(8,128)} %copy.82) | copy-start | bytes 3686404
  21.8 10.3 %copy-start.11 = (f32[75,32,128]{0,1,2:T(8,128)}, f32[75,32,128]{0,1,2:T(8,128)S(1)}, u32[]{:S(2)}) copy-start(f32[75,32,128]{0,1,2:T(8,128)S(1)} %convert_multiply_fusion) | copy-start | bytes 3686404
  21.8 10.3 %copy-start.6 = (f32[1,75,32,128]{1,2,3,0:T(8,128)S(1)}, f32[1,75,32,128]{1,2,3,0:T(8,128)}, u32[]{:S(2)}) copy-start(f32[1,75,32,128]{1,2,3,0:T(8,128)} %convert_bitcast_fusion) | copy-start | bytes 3686404
  21.8 10.3 %copy-start.7 = (f32[75,32,128]{0,1,2:T(8,128)S(1)}, f32[75,32,128]{0,1,2:T(8,128)}, u32[]{:S(2)}) copy-start(f32[75,32,128]{0,1,2:T(8,128)} %copy.81) | copy-start | bytes 3686404
  21.9 5.9 %collective-permute-start = (f32[75,32,4]{0,1,2:T(8,128)S(1)}, f32[75,32,4]{0,1,2:T(8,128)S(1)}, u32[]{:S(2)}, u32[]{:S(2)}) collective-permute-start(f32[75,32,4]{0,1,2:T(8,128)S(1)} %get-tuple-element.23), channel_id=1, source_target_pairs={{0,4},{4,8},{8,12},{12,16},{16,20},{20,24},{24,28},{28,0},{1,5},{5... | collective-permute-start | bytes 115208 | tf_op jit(solution)/shard_map/ppermute | solution.py:16
  21.9 5.8 %collective-permute-start.1 = (f32[75,32,4]{0,1,2:T(8,128)S(1)}, f32[75,32,4]{0,1,2:T(8,128)S(1)}, u32[]{:S(2)}, u32[]{:S(2)}) collective-permute-start(f32[75,32,4]{0,1,2:T(8,128)S(1)} %get-tuple-element.24), channel_id=1, source_target_pairs={{4,0},{8,4},{12,8},{16,12},{20,16},{24,20},{28,24},{0,28},{5,1},{9... | collective-permute-start | bytes 115208 | tf_op jit(solution)/shard_map/ppermute | solution.py:17
  26.2 9.9 %copy-start.21 = (s32[16384,1]{0,1:T(1,128)}, s32[16384,1]{0,1:T(1,128)S(1)}, u32[]{:S(2)}) copy-start(s32[16384,1]{0,1:T(1,128)S(1)} %compare_select_fusion) | copy-start | bytes 196612
  27.7 5.6 %copy-start.17 = (f32[75,32,4]{0,1,2:T(8,128)}, f32[75,32,4]{0,1,2:T(8,128)S(1)}, u32[]{:S(2)}) copy-start(f32[75,32,4]{0,1,2:T(8,128)S(1)} %collective-permute-done.1) | copy-start | bytes 115204
  27.9 8.9 %collective-permute-start.2 = (f32[75,4,136]{0,2,1:T(8,128)S(1)}, f32[75,4,136]{0,2,1:T(8,128)}, u32[]{:S(2)}, u32[]{:S(2)}) collective-permute-start(f32[75,4,136]{0,2,1:T(8,128)S(1)} %copy.77), channel_id=1, source_target_pairs={{0,1},{1,2},{2,3},{3,0},{4,5},{5,6},{6,7},{7,4},{8,9},{9,10},{10,1... | collective-permute-start | bytes 489608 | tf_op jit(solution)/shard_map/ppermute | solution.py:16
  32.1 8.8 %collective-permute-start.3 = (f32[75,4,136]{0,2,1:T(8,128)}, f32[75,4,136]{0,2,1:T(8,128)}, u32[]{:S(2)}, u32[]{:S(2)}) collective-permute-start(f32[75,4,136]{0,2,1:T(8,128)} %copy.78), channel_id=1, source_target_pairs={{1,0},{2,1},{3,2},{0,3},{5,4},{6,5},{7,6},{4,7},{9,8},{10,9},{11,1... | collective-permute-start | bytes 489608 | tf_op jit(solution)/shard_map/ppermute | solution.py:17
  33.4 20.8 %collective-permute-start.6 = (f32[3,75,4,136]{1,3,2,0:T(8,128)S(1)}, f32[3,75,4,136]{1,3,2,0:T(8,128)}, u32[]{:S(2)}, u32[]{:S(2)}) collective-permute-start(f32[3,75,4,136]{1,3,2,0:T(8,128)S(1)} %copy.83), channel_id=1, source_target_pairs={{0,1},{1,2},{2,3},{3,0},{4,5},{5,6},{6,7},{7,4},{8,9},{9,10},{10,1... | collective-permute-start | bytes 1468808 | tf_op jit(solution)/shard_map/ppermute | solution.py:16
  36.2 20.2 %collective-permute-start.7 = (f32[3,75,4,136]{1,3,2,0:T(8,128)}, f32[3,75,4,136]{1,3,2,0:T(8,128)}, u32[]{:S(2)}, u32[]{:S(2)}) collective-permute-start(f32[3,75,4,136]{1,3,2,0:T(8,128)} %copy.84), channel_id=1, source_target_pairs={{1,0},{2,1},{3,2},{0,3},{5,4},{6,5},{7,6},{4,7},{9,8},{10,9},{11,1... | collective-permute-start | bytes 1468808 | tf_op jit(solution)/shard_map/ppermute | solution.py:17
  41.9 15.8 %copy-start.10 = (f32[75,32,128]{0,1,2:T(8,128)S(1)}, f32[75,32,128]{0,1,2:T(8,128)}, u32[]{:S(2)}) copy-start(f32[75,32,128]{0,1,2:T(8,128)} %copy.82) | copy-start | bytes 3686404
  44.2 13.6 %copy-start.8 = (f32[75,32,128]{0,1,2:T(8,128)S(1)}, f32[75,32,128]{0,1,2:T(8,128)}, u32[]{:S(2)}) copy-start(f32[75,32,128]{0,1,2:T(8,128)} %copy.81) | copy-start | bytes 3686404
  63.5 9.9 %copy-start = (f32[75,40,135]{0,1,2:T(8,128)}, f32[75,40,135]{0,1,2:T(8,128)S(1)}, u32[]{:S(2)}) copy-start(f32[75,40,135]{0,1,2:T(8,128)S(1)} %slice_multiply_fusion.2) | copy-start | bytes 4860004
  64.0 9.3 %copy-start.2 = (f32[75,39,136]{0,1,2:T(8,128)}, f32[75,39,136]{0,1,2:T(8,128)S(1)}, u32[]{:S(2)}) copy-start(f32[75,39,136]{0,1,2:T(8,128)S(1)} %fusion.2) | copy-start | bytes 4773604
  76.8 54.8 %copy-start.18 = (f32[4,4096]{1,0:T(4,128)S(1)}, f32[4,4096]{1,0:T(4,128)}, u32[]{:S(2)}) copy-start(f32[4,4096]{1,0:T(4,128)} %param.14) | copy-start | bytes 196612
  138.6 8.2 %copy-start.14 = (f32[75,4096]{1,0:T(8,128)S(1)}, f32[75,4096]{1,0:T(8,128)}, u32[]{:S(2)}) copy-start(f32[75,4096]{1,0:T(8,128)} %param.15) | copy-start | bytes 3686404
  140.3 37.3 %all-to-all-start = ((f32[75,32,128]{2,0,1:T(8,128)}), f32[75,32,128]{2,0,1:T(8,128)S(1)}, u32[]{:S(2)}, u32[]{:S(2)}) async-start(f32[75,32,128]{2,0,1:T(8,128)} %copy.89), calls=%async_computation | async-start | bytes 2621440 | tf_op jit(solution)/shard_map/all_to_all | solution.py:81
  205.6 35.4 %all-to-all-start.1 = ((f32[32,75,128]{2,1,0:T(8,128)}), f32[32,75,128]{2,1,0:T(8,128)S(1)}, u32[]{:S(2)}, u32[]{:S(2)}) async-start(f32[32,75,128]{2,1,0:T(8,128)} %copy.93), calls=%async_computation.1 | async-start | bytes 2621440 | tf_op jit(solution)/shard_map/all_to_all | solution.py:85
  330.9 5.9 %collective-permute-start.8 = (f32[75,32,4]{0,1,2:T(8,128)S(1)}, f32[75,32,4]{0,1,2:T(8,128)S(1)}, u32[]{:S(2)}, u32[]{:S(2)}) collective-permute-start(f32[75,32,4]{0,1,2:T(8,128)S(1)} %copy.113), channel_id=1, source_target_pairs={{0,4},{4,8},{8,12},{12,16},{16,20},{20,24},{24,28},{28,0},{1,5},{5... | collective-permute-start | bytes 115208 | tf_op jit(solution)/shard_map/ppermute | solution.py:16
  332.3 7.3 %collective-permute-start.9 = (f32[75,32,4]{0,1,2:T(8,128)S(1)}, f32[75,32,4]{0,1,2:T(8,128)S(1)}, u32[]{:S(2)}, u32[]{:S(2)}) collective-permute-start(f32[75,32,4]{0,1,2:T(8,128)S(1)} %copy.114), channel_id=1, source_target_pairs={{4,0},{8,4},{12,8},{16,12},{20,16},{24,20},{28,24},{0,28},{5,1},{9... | collective-permute-start | bytes 115208 | tf_op jit(solution)/shard_map/ppermute | solution.py:17
  341.1 8.8 %collective-permute-start.10 = (f32[75,4,136]{0,2,1:T(8,128)S(1)}, f32[75,4,136]{0,2,1:T(8,128)S(1)}, u32[]{:S(2)}, u32[]{:S(2)}) collective-permute-start(f32[75,4,136]{0,2,1:T(8,128)S(1)} %copy.99), channel_id=1, source_target_pairs={{0,1},{1,2},{2,3},{3,0},{4,5},{5,6},{6,7},{7,4},{8,9},{9,10},{10,1... | collective-permute-start | bytes 489608 | tf_op jit(solution)/shard_map/ppermute | solution.py:16
  344.7 7.2 %collective-permute-start.11 = (f32[75,4,136]{0,2,1:T(8,128)S(1)}, f32[75,4,136]{0,2,1:T(8,128)S(1)}, u32[]{:S(2)}, u32[]{:S(2)}) collective-permute-start(f32[75,4,136]{0,2,1:T(8,128)S(1)} %copy.100), channel_id=1, source_target_pairs={{1,0},{2,1},{3,2},{0,3},{5,4},{6,5},{7,6},{4,7},{9,8},{10,9},{11,1... | collective-permute-start | bytes 489608 | tf_op jit(solution)/shard_map/ppermute | solution.py:17
  351.9 3.3 copy-start.3
  361.2 3.0 copy-start.5
  361.2 3.0 copy-start.12
  (5 other events, 10.1 us)
